TPU v7x, 32 devices: a whole 2x2x4 slice. The times are simulated.
32 devices in a mesh: blk: 4 (over y, x), strata: 8 (over z, core).
Axes of the slice: x: 2, y: 2, z: 4, core: 2. Of those that a mesh axis runs over, the one named last changes fastest.
Arguments:
- user_factors: bfloat16 [4096, 256], P('blk'), may hold values from -1.5 to 1.5
- item_factors: bfloat16 [8192, 256], P(('blk', 'strata')), may hold values from -1.5 to 1.5
- ratings: bfloat16 [4, 4, 8, 8, 128, 128], P('blk', None, 'strata'), may hold values from -6 to 6
- tile_user: int32 [4, 4, 8, 8], P('blk', None, 'strata'), may hold values from 0 to 7
- tile_item: int32 [4, 4, 8, 8], P('blk', None, 'strata'), may hold values from 0 to 1
- tile_count: int32 [4, 4, 8], P('blk', None, 'strata'), may hold values from 1 to 8, 40 in all within a row
Outputs:
- user_grad: float32 [4096, 256], P('blk')
- item_grad: float32 [8192, 256], P(('blk', 'strata'))
Inputs may be any that keep to these rules, and one draw needn't show every extreme that they name: `tile_count`: for each user block and panel index, the counts over the strata are uneven and one of them equals 8.
All inputs are finite; a program needn't handle non-finite values.
Results may differ from a plain program's by a relative error of at most 0.0012.
Values may be sent and summed in bfloat16 or wider, within the bound.
A program may use at most 64 MiB of HBM per device.

v0:
```python
import jax
import jax.numpy as jnp
from jax import lax
from jax.sharding import PartitionSpec as P


def tile_terms(user_tiles, panel_tiles, rating_tiles, rows, cols, count):
    slots = rating_tiles.shape[0]
    tile = rating_tiles.shape[-1]
    picked_users = jnp.take(user_tiles, rows, axis=0)
    picked_items = jnp.take(panel_tiles, cols, axis=0)
    predicted = jnp.einsum(
        "kar,kbr->kab", picked_users, picked_items, preferred_element_type=jnp.float32
    )
    live = (jnp.arange(slots) < count).astype(jnp.float32)
    residue = ((predicted - rating_tiles.astype(jnp.float32)) * live[:, None, None]).astype(
        jnp.bfloat16
    )
    user_part = (
        jnp.einsum("kab,kbr->kar", residue, picked_items, preferred_element_type=jnp.float32) / tile
    )
    item_part = (
        jnp.einsum("kab,kar->kbr", residue, picked_users, preferred_element_type=jnp.float32) / tile
    )
    user_hot = (rows[:, None] == jnp.arange(user_tiles.shape[0])[None, :]).astype(jnp.float32)
    item_hot = (cols[:, None] == jnp.arange(panel_tiles.shape[0])[None, :]).astype(jnp.float32)
    user_sum = jnp.einsum("ku,kar->uar", user_hot, user_part, precision=lax.Precision.HIGHEST)
    item_sum = jnp.einsum("kp,kbr->pbr", item_hot, item_part, precision=lax.Precision.HIGHEST)
    return (user_sum, item_sum)


def settle_early(user_total, early):
    return (user_total, early)


def body(user_factors, item_factors, ratings, tile_user, tile_item, tile_count):
    steps = lax.axis_size("blk")
    tile = ratings.shape[-1]
    rank = user_factors.shape[1]
    panel_rows = item_factors.shape[0]
    user_tiles = user_factors.reshape(-1, tile, rank)
    rating_sets = ratings[0, :, 0]
    row_sets = tile_user[0, :, 0]
    col_sets = tile_item[0, :, 0]
    count_sets = tile_count[0, :, 0]
    user_total = jnp.zeros(user_tiles.shape, jnp.float32)
    early = None
    gathered = lax.all_gather(item_factors, "blk", axis=0, tiled=True)
    pieces = []
    for source in range(steps):
        panel = gathered[source * panel_rows : (source + 1) * panel_rows]
        rating_tiles = lax.dynamic_index_in_dim(rating_sets, source, 0, keepdims=False)
        rows = lax.dynamic_index_in_dim(row_sets, source, 0, keepdims=False)
        cols = lax.dynamic_index_in_dim(col_sets, source, 0, keepdims=False)
        count = lax.dynamic_index_in_dim(count_sets, source, 0, keepdims=False)
        user_part, item_part = tile_terms(
            user_tiles, panel.reshape(-1, tile, rank), rating_tiles, rows, cols, count
        )
        user_total = user_total + user_part
        pieces.append(item_part.reshape(panel_rows, rank))
        user_total, early = settle_early(user_total, early)
    item_grad = lax.psum_scatter(
        jnp.concatenate(pieces, axis=0), "blk", scatter_dimension=0, tiled=True
    )
    user_grad = lax.psum(user_total, "strata")
    return (user_grad.reshape(-1, rank), item_grad)


def solution(mesh):
    in_specs = (
        P("blk", None),
        P(("blk", "strata"), None),
        P("blk", None, "strata", None, None, None),
        P("blk", None, "strata", None),
        P("blk", None, "strata", None),
        P("blk", None, "strata"),
    )
    out_specs = (P("blk", None), P(("blk", "strata"), None))
    return jax.shard_map(body, mesh=mesh, in_specs=in_specs, out_specs=out_specs, check_vma=False)
```

profile of v0, /device:TPU:0, one launch (start us, length us, event | category | flops | bytes accessed | tf_op | source)
XLA Modules:
  0.0 119.4 jit_solution(5555860137044684791)
XLA Ops:
  8.0 0.0 copy-start
  8.0 0.0 copy-start.16
  8.0 0.0 all-reduce.2.cloned.1.call-start
  8.1 0.8 compare_and_fusion.1
  8.8 0.0 copy-done.16
  8.8 0.0 copy-start.17
  8.9 0.7 copy-done.17
  9.5 11.8 %all_gather.3 = bf16[1024,256]{1,0:T(8,128)(2,1)S(1)} all-gather(bf16[256,256]{1,0:T(8,128)(2,1)} %param.11), channel_id=1, replica_groups=mesh['blk'=4,'strata'=8] {'blk'}, dimensions={0}, use_global_device_ids=true | all-gather | bytes 655360 | tf_op jit(solution)/shard_map/all_gather | solution.py:48
  21.4 0.6 copy-done.18
  22.0 0.6 fusion.78
  22.7 0.6 compare_convert_fusion.1
  23.3 0.0 copy-done
  23.3 1.4 %gather_fusion.4 = bf16[8,128,256]{2,1,0:T(8,128)(2,1)} fusion(bf16[8,128,256]{2,1,0:T(8,128)(2,1)S(1)} %bitcast.100, s32[1024]{0:T(1024)S(1)} %get-tuple-element.49), kind=kCustom, calls=%fused_computation.3.clone | custom fusion | bytes 1048608 | tf_op jit(solution)/shard_map/jit(_take)/gather | solution.py:10
  24.7 0.6 gather_fusion.6
  25.3 0.7 compare_convert_fusion
  25.9 0.6 gather_fusion.2
  26.5 0.0 copy-start.2
  26.5 0.7 compare_convert_fusion.2
  27.2 0.6 gather_fusion
  27.8 0.0 copy-start.5
  27.8 0.6 compare_convert_fusion.3
  28.5 1.4 %gather_fusion.1 = bf16[8,128,256]{2,1,0:T(8,128)(2,1)} fusion(bf16[2,128,256]{2,1,0:T(8,128)(2,1)S(1)} %bitcast.106, s32[1024]{0:T(1024)S(1)} %get-tuple-element.55), kind=kCustom, calls=%fused_computation.1.clone | custom fusion | bytes 1048608 | tf_op jit(solution)/shard_map/jit(_take)/gather | solution.py:11
  29.9 0.0 copy-done.5
  29.9 1.5 %fusion.4 = bf16[8,128,128]{2,1,0:T(8,128)(2,1)S(1)} fusion(f32[8]{0:T(128)S(1)} %compare_convert_fusion.3, bf16[1,4,1,8,128,128]{5,4,3,2,1,0:T(8,128)(2,1)} %param.12, bf16[8,128,256]{2,1,0:T(8,128)(2,1)S(1)} %gather_fusion, pred[8]{0:T(512)(128)(4,1)S(1)} %get-tuple-element.42, bf16[8,128,256]{2,1,0:T(8,128)(2,1)} %gather_fusion.1, ...), kind=kOutput, calls=%fused_computation.19 | convolution fusion | flops 68157440 | bytes 1572912 | tf_op jit(solution)/shard_map/kar,kbr->kab/dot_general | solution.py:12
  31.4 0.0 copy-start.10
  31.4 1.5 %fusion.22 = f32[8,128,256]{2,1,0:T(8,128)S(1)} fusion(bf16[8,128,128]{2,1,0:T(8,128)(2,1)S(1)} %fusion.4, bf16[8,128,256]{2,1,0:T(8,128)(2,1)} %gather_fusion.1, pred[8]{0:T(512)(128)(4,1)S(1)} %get-tuple-element.36), kind=kOutput, calls=%fused_computation.54 | convolution fusion | flops 67371008 | bytes 1835016 | tf_op jit(solution)/shard_map/kab,kbr->kar/dot_general | solution.py:20
  32.9 1.4 %gather_fusion.3 = bf16[8,128,256]{2,1,0:T(8,128)(2,1)} fusion(bf16[2,128,256]{2,1,0:T(8,128)(2,1)S(1)} %bitcast.105, s32[1024]{0:T(1024)S(1)} %get-tuple-element.54), kind=kCustom, calls=%fused_computation.5.clone | custom fusion | bytes 1048608 | tf_op jit(solution)/shard_map/jit(_take)/gather | solution.py:11
  34.3 1.6 %fusion.5 = bf16[8,128,128]{2,1,0:T(8,128)(2,1)S(1)} fusion(f32[8]{0:T(128)S(1)} %compare_convert_fusion.2, bf16[1,4,1,8,128,128]{5,4,3,2,1,0:T(8,128)(2,1)} %param.12, bf16[8,128,256]{2,1,0:T(8,128)(2,1)S(1)} %gather_fusion.2, pred[8]{0:T(512)(128)(4,1)S(1)} %get-tuple-element.40, bf16[8,128,256]{2,1,0:T(8,128)(2,1)} %gather_fusion.3, ...), kind=kOutput, calls=%fused_computation.20 | convolution fusion | flops 68157440 | bytes 1572912 | tf_op jit(solution)/shard_map/kar,kbr->kab/dot_general | solution.py:12
  35.8 0.4 fusion.24
  36.2 0.3 copy-done.12
  36.5 1.4 %gather_fusion.5 = bf16[8,128,256]{2,1,0:T(8,128)(2,1)} fusion(bf16[2,128,256]{2,1,0:T(8,128)(2,1)S(1)} %bitcast.104, s32[1024]{0:T(1024)S(1)} %get-tuple-element.53), kind=kCustom, calls=%fused_computation.6.clone | custom fusion | bytes 1048608 | tf_op jit(solution)/shard_map/jit(_take)/gather | solution.py:11
  37.9 1.7 %fusion.6 = bf16[8,128,128]{2,1,0:T(8,128)(2,1)S(1)} fusion(f32[8]{0:T(128)S(1)} %compare_convert_fusion.1, bf16[1,4,1,8,128,128]{5,4,3,2,1,0:T(8,128)(2,1)} %param.12, bf16[8,128,256]{2,1,0:T(8,128)(2,1)} %gather_fusion.4, pred[8]{0:T(512)(128)(4,1)S(1)} %get-tuple-element.38, bf16[8,128,256]{2,1,0:T(8,128)(2,1)} %gather_fusion.5, ...), kind=kOutput, calls=%fused_computation.21 | convolution fusion | flops 68157440 | bytes 1572912 | tf_op jit(solution)/shard_map/kar,kbr->kab/dot_general | solution.py:12
  39.6 0.0 copy-start.14
  39.7 1.3 %fusion.26 = f32[8,128,256]{2,1,0:T(8,128)} fusion(bf16[8,128,128]{2,1,0:T(8,128)(2,1)S(1)} %fusion.6, bf16[8,128,256]{2,1,0:T(8,128)(2,1)S(1)} %copy-done.9, pred[8]{0:T(512)(128)(4,1)S(1)} %get-tuple-element.32), kind=kOutput, calls=%fused_computation.58 | convolution fusion | flops 67371008 | bytes 1835016 | tf_op jit(solution)/shard_map/kab,kbr->kar/dot_general | solution.py:20
  41.0 1.4 %gather_fusion.7 = bf16[8,128,256]{2,1,0:T(8,128)(2,1)} fusion(bf16[2,128,256]{2,1,0:T(8,128)(2,1)S(1)} %bitcast.103, s32[1024]{0:T(1024)S(1)} %get-tuple-element.52), kind=kCustom, calls=%fused_computation.7.clone | custom fusion | bytes 1048608 | tf_op jit(solution)/shard_map/jit(_take)/gather | solution.py:11
  42.4 1.5 %fusion.7 = bf16[8,128,128]{2,1,0:T(8,128)(2,1)S(1)} fusion(f32[8]{0:T(128)S(1)} %compare_convert_fusion, bf16[1,4,1,8,128,128]{5,4,3,2,1,0:T(8,128)(2,1)} %param.12, bf16[8,128,256]{2,1,0:T(8,128)(2,1)S(1)} %gather_fusion.6, pred[8]{0:T(512)(128)(4,1)S(1)} %get-tuple-element.6, bf16[8,128,256]{2,1,0:T(8,128)(2,1)} %gather_fusion.7, ...), kind=kOutput, calls=%fused_computation.22 | convolution fusion | flops 68157440 | bytes 1572912 | tf_op jit(solution)/shard_map/kar,kbr->kab/dot_general | solution.py:12
  43.9 0.4 fusion.28
  44.3 1.2 fusion.12
  45.5 0.0 copy-start.1
  45.5 1.2 convolution_add_fusion.2
  46.7 0.0 copy-done.1
  46.7 1.2 convolution_add_fusion.1
  47.9 1.2 convolution_add_fusion
  49.1 1.3 %copy.8 = f32[8,128,256]{2,1,0:T(8,128)} copy(f32[8,128,256]{2,0,1:T(8,128)S(1)} %convolution_add_fusion) | data formatting | bytes 2097152 | tf_op jit(solution)/shard_map/add | solution.py:59
  50.4 0.0 all-reduce.2.cloned.1.call-update
  50.4 0.2 reduce-scatter.2.cloned.1.call-start
  50.6 0.8 copy-done.4
  51.4 0.1 copy-done.15
  51.5 0.4 fusion.25
  51.9 0.4 fusion.27
  52.2 0.7 copy-done.3
  52.9 0.1 copy-done.13
  53.0 0.4 fusion.23
  53.3 0.7 copy-done.6
  54.0 0.1 copy-done.11
  54.1 0.4 fusion.21
  54.4 1.2 fusion.9
  55.6 1.2 fusion.8
  56.8 1.2 fusion.10
  58.1 1.2 fusion.11
  59.3 1.0 pad_maximum_fusion
  60.3 0.0 reduce-scatter.2.cloned.1.call-update
  60.3 49.4 %all-reduce.2.cloned.1.call-done = f32[1024,256]{1,0:T(8,128)} async-done(((f32[1024,256]{1,0:T(8,128)}), f32[1024,256]{1,0:T(8,128)}) %all-reduce.2.cloned.1.call-update) | async-done | bytes 1048592 | tf_op jit(solution)/shard_map/psum | solution.py:65
  109.7 2.3 %copy.38 = f32[1024,256]{1,0:T(8,128)} copy(f32[1024,256]{1,0:T(8,128)} %all-reduce.2.cloned.1.call-done) | data formatting | bytes 2097152
  (30 shorter events, 0.2 us)
Async XLA Ops:
  8.0 15.3 %copy-start = (bf16[1024,256]{1,0:T(8,128)(2,1)S(1)}, bf16[1024,256]{1,0:T(8,128)(2,1)}, u32[]{:S(2)}) copy-start(bf16[1024,256]{1,0:T(8,128)(2,1)} %param.10) | copy-start | bytes 1572868
  8.0 0.8 copy-start.16
  8.0 101.7 %all-reduce.2.cloned.1.call-start = ((), (), s32[]{:S(2)}) async-start(), calls=%async_computation.1 | async-start | bytes 2097152 | tf_op jit(solution)/shard_map/psum | solution.py:65
  8.8 0.7 copy-start.17
  21.4 0.7 copy-start.18
  26.5 7.7 %copy-start.2 = (bf16[8,128,256]{2,1,0:T(8,128)(2,1)}, bf16[8,128,256]{2,1,0:T(8,128)(2,1)S(1)}, u32[]{:S(2)}) copy-start(bf16[8,128,256]{2,1,0:T(8,128)(2,1)S(1)} %gather_fusion.2) | copy-start | bytes 1572868
  27.8 2.0 %copy-start.5 = (bf16[8,128,256]{2,1,0:T(8,128)(2,1)}, bf16[8,128,256]{2,1,0:T(8,128)(2,1)S(1)}, u32[]{:S(2)}) copy-start(bf16[8,128,256]{2,1,0:T(8,128)(2,1)S(1)} %gather_fusion) | copy-start | bytes 1572868
  31.4 1.5 %copy-start.10 = (bf16[8,128,128]{2,1,0:T(8,128)(2,1)}, bf16[8,128,128]{2,1,0:T(8,128)(2,1)S(1)}, u32[]{:S(2)}) copy-start(bf16[8,128,128]{2,1,0:T(8,128)(2,1)S(1)} %fusion.4) | copy-start | bytes 786436
  34.3 1.6 %copy-start.8 = (bf16[8,128,256]{2,1,0:T(8,128)(2,1)S(1)}, bf16[8,128,256]{2,1,0:T(8,128)(2,1)}, u32[]{:S(2)}) copy-start(bf16[8,128,256]{2,1,0:T(8,128)(2,1)} %gather_fusion.3) | copy-start | bytes 1572868
  35.8 0.7 copy-start.12
  37.9 1.7 %copy-start.9 = (bf16[8,128,256]{2,1,0:T(8,128)(2,1)S(1)}, bf16[8,128,256]{2,1,0:T(8,128)(2,1)}, u32[]{:S(2)}) copy-start(bf16[8,128,256]{2,1,0:T(8,128)(2,1)} %gather_fusion.5) | copy-start | bytes 1572868
  39.6 1.4 %copy-start.14 = (bf16[8,128,128]{2,1,0:T(8,128)(2,1)}, bf16[8,128,128]{2,1,0:T(8,128)(2,1)S(1)}, u32[]{:S(2)}) copy-start(bf16[8,128,128]{2,1,0:T(8,128)(2,1)S(1)} %fusion.6) | copy-start | bytes 786436
  42.4 1.6 %copy-start.7 = (bf16[8,128,256]{2,1,0:T(8,128)(2,1)S(1)}, bf16[8,128,256]{2,1,0:T(8,128)(2,1)}, u32[]{:S(2)}) copy-start(bf16[8,128,256]{2,1,0:T(8,128)(2,1)} %gather_fusion.7) | copy-start | bytes 1572868
  45.5 1.2 %copy-start.1 = (f32[8,128,256]{2,1,0:T(8,128)S(1)}, f32[8,128,256]{2,1,0:T(8,128)}, u32[]{:S(2)}) copy-start(f32[8,128,256]{2,1,0:T(8,128)} %fusion.26) | copy-start | bytes 3145732
  50.4 1.0 copy-start.4
  50.4 1.1 copy-start.15
  50.4 59.3 %reduce-scatter.2.cloned.1.call-start = ((), (), s32[]{:S(2)}) async-start(), calls=%async_computation.2 | async-start | bytes 1310720 | tf_op jit(solution)/shard_map/reduce_scatter | solution.py:62
  51.9 1.0 copy-start.3
  51.9 1.1 copy-start.13
  53.0 1.0 copy-start.6
  53.0 1.1 copy-start.11
Sparse Core Ops, SparseCore 0:
  50.5 59.1 all-reduce.1
Sparse Core Ops, SparseCore 1:
  60.4 27.9 reduce-scatter.1
where the time goes:
time: 120 us; the launch traced here: 119 us
  waiting for transfers between devices  49.4 us (41%)
  matrix products  20.7 us (17%)
  local copies, waits for them, and re-layouts  16.9 us (14%)
  between operations  15.9 us (13%)
  blocking collectives  11.8 us (10%)
  other arithmetic  4.39 us (4%)
    psum x1, waiting for transfers between devices, body(): user_grad = lax.psum(user_total, 'strata')  49.4 us
    all_gather x1, blocking collectives, body(): gathered = lax.all_gather(item_factors, 'blk', axis=0, tiled=True)  11.8 us
    dot_general x4, matrix products, tile_terms(): jnp.einsum('kar,kbr->kab', picked_users, picked_items, preferred_element_...  6.31 us
    unnamed x39, local copies, waits for them, and re-layouts  6.27 us
    gather x4, local copies, waits for them, and re-layouts, tile_terms(): picked_items = jnp.take(panel_tiles, cols, axis=0)  5.5 us
    dot_general x4, matrix products, tile_terms(): jnp.einsum('ku,kar->uar', user_hot, user_part, precision=lax.Precision.HI...  4.7 us
    dot_general x4, matrix products, tile_terms(): jnp.einsum('kp,kbr->pbr', item_hot, item_part, precision=lax.Precision.HI...  4.68 us
    dot_general x4, matrix products, tile_terms(): jnp.einsum('kab,kbr->kar', residue, picked_items, preferred_element_type=...  3.57 us
  transfers between devices with their start and end apart: 2, of which 1 were waited for; matrix products, arithmetic and copies ran while one was open for 6% of the time, Pallas kernels for 0%

commit v1 on v0

--- a/solution.py
+++ b/solution.py
@@ -45,7 +45,30 @@
     count_sets = tile_count[0, :, 0]
     user_total = jnp.zeros(user_tiles.shape, jnp.float32)
     early = None
-    gathered = lax.all_gather(item_factors, "blk", axis=0, tiled=True)
+
+    def streams_run(inner_x):
+        aux, v_next, z_new = (lax.axis_size("blk"), lax.axis_index("blk"), inner_x.shape[0])
+        column = [(w, (w + 1) % aux) for w in range(aux)]
+        history = [(w, (w - 1) % aux) for w in range(aux)]
+        p_next = jnp.zeros((*inner_x.shape[:0], aux * z_new, *inner_x.shape[1:]), inner_x.dtype)
+        p_next = lax.dynamic_update_slice_in_dim(p_next, inner_x, v_next * z_new, axis=0)
+        plain = y = inner_x
+        arr_next = aux // 2
+        m = 1
+        while m < arr_next + 1:
+            plain = lax.ppermute(plain, "blk", perm=column)
+            p_next = lax.dynamic_update_slice_in_dim(
+                p_next, plain, (v_next - m) % aux * z_new, axis=0
+            )
+            if m < aux - arr_next:
+                y = lax.ppermute(y, "blk", perm=history)
+                p_next = lax.dynamic_update_slice_in_dim(
+                    p_next, y, (v_next + m) % aux * z_new, axis=0
+                )
+            m = m + 1
+        return p_next
+
+    gathered = streams_run(item_factors)
     pieces = []
     for source in range(steps):
         panel = gathered[source * panel_rows : (source + 1) * panel_rows]

time: 120 us -> 130 us (1.083)
  blocking collectives: 11.8 us -> 0 us
  local copies, waits for them, and re-layouts: 16.9 us -> 22.7 us
  waiting for transfers between devices: 49.4 us -> 55 us
  starting transfers between devices: 0.26 us -> 5.28 us
  matrix products: 20.7 us -> 24.4 us
  other arithmetic: 4.39 us -> 5.9 us
    all_gather x1 -> x0, blocking collectives: 11.8 us -> none  [body(): gathered = lax.all_gather(item_factors, 'blk', axis=0, tiled=True)]
    unnamed x39 -> x67, local copies, waits for them, and re-layouts: 6.27 us -> 11.7 us
    ppermute x0 -> x3, starting transfers between devices: none -> 5.02 us  [the longest x2 3.99 us: streams_run(): plain = lax.ppermute(plain, 'blk', perm=column)]
    ppermute x0 -> x3, waiting for transfers between devices: none -> 4.82 us  [the longest x2 4.82 us: streams_run(): plain = lax.ppermute(plain, 'blk', perm=column)]
    dot_general x4, matrix products: 1.42 us -> 5.07 us  [tile_terms(): jnp.einsum('kab,kar->kbr', residue, picked_users, preferred_element_type=...]
    gather x4, local copies, waits for them, and re-layouts: 5.5 us -> 3.11 us  [tile_terms(): picked_items = jnp.take(panel_tiles, cols, axis=0)]
    convert_element_type x4, other arithmetic: 2.57 us -> 4.22 us  [tile_terms(): live = (jnp.arange(slots) < count).astype(jnp.float32)]
    squeeze x1, local copies, waits for them, and re-layouts: 0.01 us -> 1.32 us  [body(): cols = lax.dynamic_index_in_dim(col_sets, source, 0, keepdims=False)]
  transfers between devices with their start and end apart: 2 -> 5, of which waited for: 1 -> 2; matrix products, arithmetic and copies ran while one was open for 6% -> 13% of each run, Pallas kernels for 0% -> 0%
where the time goes in v1:
time: 130 us; the launch traced here: 129 us
  waiting for transfers between devices  55 us (42%)
  matrix products  24.4 us (19%)
  local copies, waits for them, and re-layouts  22.7 us (17%)
  between operations  16 us (12%)
  other arithmetic  5.9 us (5%)
  starting transfers between devices  5.28 us (4%)
    psum x1, waiting for transfers between devices, body(): user_grad = lax.psum(user_total, 'strata')  50.2 us
    unnamed x67, local copies, waits for them, and re-layouts  11.7 us
    dot_general x4, matrix products, tile_terms(): jnp.einsum('kar,kbr->kab', picked_users, picked_items, preferred_element_...  5.5 us
    dot_general x4, matrix products, tile_terms(): jnp.einsum('kab,kar->kbr', residue, picked_users, preferred_element_type=...  5.07 us
    ppermute x2, waiting for transfers between devices, streams_run(): plain = lax.ppermute(plain, 'blk', perm=column)  4.82 us
    dot_general x4, matrix products, tile_terms(): jnp.einsum('ku,kar->uar', user_hot, user_part, precision=lax.Precision.HI...  4.69 us
    dot_general x4, matrix products, tile_terms(): jnp.einsum('kp,kbr->pbr', item_hot, item_part, precision=lax.Precision.HI...  4.67 us
    dot_general x4, matrix products, tile_terms(): jnp.einsum('kab,kbr->kar', residue, picked_items, preferred_element_type=...  4.46 us
  transfers between devices with their start and end apart: 5, of which 2 were waited for; matrix products, arithmetic and copies ran while one was open for 13% of the time, Pallas kernels for 0%

profile of v1, /device:TPU:0, one launch (start us, length us, event | category | flops | bytes accessed | tf_op | source)
XLA Modules:
  0.0 129.3 jit_solution(7522659022180584328)
XLA Ops:
  8.0 0.0 all-reduce.2.cloned.1.call-start
  8.1 3.0 %collective-permute-start = (bf16[256,256]{1,0:T(8,128)(2,1)}, bf16[256,256]{1,0:T(8,128)(2,1)S(1)}, u32[]{:S(2)}, u32[]{:S(2)}) collective-permute-start(bf16[256,256]{1,0:T(8,128)(2,1)} %param.11), channel_id=1, source_target_pairs={{0,8},{8,16},{16,24},{24,0},{1,9},{9,17},{17,25},{25,1},{2,10},{10... | collective-permute-start | bytes 393224 | tf_op jit(solution)/shard_map/ppermute | solution.py:59
  11.0 1.0 collective-permute-start.1
  12.1 1.3 %slice_bitcast_fusion.6 = (s32[8]{0:T(128)S(1)}, s32[8]{0:T(128)}, s32[8]{0:T(128)}, s32[8]{0:T(128)}) fusion(s32[1,4,1,8]{3,2,1,0:T(1,128)} %param.14), kind=kLoop, calls=%fused_computation.127 | loop fusion | bytes 256 | tf_op jit(solution)/shard_map/jit(dynamic_index_in_dim)/squeeze | solution.py:77
  13.4 0.6 compare_and_fusion
  14.0 0.5 slice_bitcast_fusion.1
  14.6 0.6 copy-done.11
  15.2 0.7 fusion.78
  15.9 1.2 compare_convert_fusion.2
  17.1 0.7 compare_convert_fusion.1
  17.9 0.9 copy-done.10
  18.7 1.2 compare_convert_fusion
  19.9 1.2 compare_convert_fusion.3
  21.1 1.4 %gather_fusion.2 = bf16[8,128,256]{2,1,0:T(8,128)(2,1)} fusion(bf16[8,128,256]{2,1,0:T(8,128)(2,1)S(1)} %bitcast.99, s32[1024]{0:T(1024)S(1)} %pad_clamp_fusion.5), kind=kCustom, calls=%fused_computation.2.clone | custom fusion | bytes 1048608 | tf_op jit(solution)/shard_map/jit(_take)/gather | solution.py:10
  22.5 0.6 gather_fusion.4
  23.1 0.6 gather_fusion.6
  23.7 1.4 %gather_fusion = bf16[8,128,256]{2,1,0:T(8,128)(2,1)} fusion(bf16[8,128,256]{2,1,0:T(8,128)(2,1)S(1)} %bitcast.98, s32[1024]{0:T(1024)S(1)} %pad_clamp_fusion.7), kind=kCustom, calls=%fused_computation.clone | custom fusion | bytes 1048608 | tf_op jit(solution)/shard_map/jit(_take)/gather | solution.py:10
  25.0 1.0 collective-permute-start.2
  26.1 4.8 %collective-permute-done.2 = bf16[256,256]{1,0:T(8,128)(2,1)S(1)} collective-permute-done((bf16[256,256]{1,0:T(8,128)(2,1)S(1)}, bf16[256,256]{1,0:T(8,128)(2,1)S(1)}, u32[]{:S(2)}, u32[]{:S(2)}) %collective-permute-start.2) | collective-permute-done | bytes 131104 | tf_op jit(solution)/shard_map/ppermute | solution.py:59
  31.0 0.6 gather_fusion.5
  31.6 1.3 %fusion.6 = bf16[8,128,128]{2,1,0:T(8,128)(2,1)S(1)} fusion(f32[8]{0:T(128)S(1)} %compare_convert_fusion.1, bf16[1,4,1,8,128,128]{5,4,3,2,1,0:T(8,128)(2,1)} %param.12, bf16[8,128,256]{2,1,0:T(8,128)(2,1)S(1)} %gather_fusion.4, pred[8]{0:T(512)(128)(4,1)S(1)} %get-tuple-element.52, bf16[8,128,256]{2,1,0:T(8,128)(2,1)S(1)} %gather_fusion.5, ...), kind=kOutput, calls=%fused_computation.21 | convolution fusion | flops 68157440 | bytes 1572912 | tf_op jit(solution)/shard_map/kar,kbr->kab/dot_general | solution.py:12
  32.9 1.0 fusion.25
  34.0 1.4 %fusion.26 = f32[8,128,256]{2,1,0:T(8,128)} fusion(bf16[8,128,128]{2,1,0:T(8,128)(2,1)S(1)} %fusion.6, bf16[8,128,256]{2,1,0:T(8,128)(2,1)S(1)} %gather_fusion.5, pred[8]{0:T(512)(128)(4,1)S(1)} %copy-done.25), kind=kOutput, calls=%fused_computation.58 | convolution fusion | flops 67371008 | bytes 1835016 | tf_op jit(solution)/shard_map/kab,kbr->kar/dot_general | solution.py:20
  35.3 0.6 gather_fusion.3
  35.9 0.4 copy-done.7
  36.4 0.3 copy-done.22
  36.6 1.3 %fusion.5 = bf16[8,128,128]{2,1,0:T(8,128)(2,1)S(1)} fusion(f32[8]{0:T(128)S(1)} %copy-done.31, bf16[1,4,1,8,128,128]{5,4,3,2,1,0:T(8,128)(2,1)} %param.12, bf16[8,128,256]{2,1,0:T(8,128)(2,1)S(1)} %copy-done.7, pred[8]{0:T(512)(128)(4,1)S(1)} %copy-done.23, bf16[8,128,256]{2,1,0:T(8,128)(2,1)S(1)} %gather_fusion.3, pred[8]{0:T(512)(128)(4,1)S(1)} %copy-done.22), kind=kOutput, calls=%fused_computation.20 | convolution fusion | flops 68157440 | bytes 1572912 | tf_op jit(solution)/shard_map/kar,kbr->kab/dot_general | solution.py:12
  38.0 1.3 %fusion.23 = f32[8,128,256]{2,1,0:T(8,128)} fusion(bf16[8,128,128]{2,1,0:T(8,128)(2,1)S(1)} %fusion.5, bf16[8,128,256]{2,1,0:T(8,128)(2,1)S(1)} %copy-done.7, pred[8]{0:T(512)(128)(4,1)S(1)} %copy-done.23), kind=kOutput, calls=%fused_computation.55 | convolution fusion | flops 67371008 | bytes 1835016 | tf_op jit(solution)/shard_map/kab,kar->kbr/dot_general | solution.py:23
  39.3 1.3 %fusion.24 = f32[8,128,256]{2,1,0:T(8,128)} fusion(bf16[8,128,128]{2,1,0:T(8,128)(2,1)S(1)} %fusion.5, bf16[8,128,256]{2,1,0:T(8,128)(2,1)S(1)} %gather_fusion.3, pred[8]{0:T(512)(128)(4,1)S(1)} %copy-done.22), kind=kOutput, calls=%fused_computation.56 | convolution fusion | flops 67371008 | bytes 1835016 | tf_op jit(solution)/shard_map/kab,kbr->kar/dot_general | solution.py:20
  40.6 0.6 gather_fusion.1
  41.3 0.4 copy-done.6
  41.7 0.3 copy-done.20
  41.9 0.1 copy-done.32
  42.0 1.3 %fusion.4 = bf16[8,128,128]{2,1,0:T(8,128)(2,1)S(1)} fusion(f32[8]{0:T(128)S(1)} %copy-done.32, bf16[1,4,1,8,128,128]{5,4,3,2,1,0:T(8,128)(2,1)} %param.12, bf16[8,128,256]{2,1,0:T(8,128)(2,1)S(1)} %copy-done.6, pred[8]{0:T(512)(128)(4,1)S(1)} %copy-done.21, bf16[8,128,256]{2,1,0:T(8,128)(2,1)S(1)} %gather_fusion.1, pred[8]{0:T(512)(128)(4,1)S(1)} %copy-done.20), kind=kOutput, calls=%fused_computation.19 | convolution fusion | flops 68157440 | bytes 1572912 | tf_op jit(solution)/shard_map/kar,kbr->kab/dot_general | solution.py:12
  43.3 1.4 %fusion.21 = f32[8,128,256]{2,1,0:T(8,128)} fusion(bf16[8,128,128]{2,1,0:T(8,128)(2,1)S(1)} %fusion.4, bf16[8,128,256]{2,1,0:T(8,128)(2,1)S(1)} %copy-done.6, pred[8]{0:T(512)(128)(4,1)S(1)} %copy-done.21), kind=kOutput, calls=%fused_computation.53 | convolution fusion | flops 67371008 | bytes 1835016 | tf_op jit(solution)/shard_map/kab,kar->kbr/dot_general | solution.py:23
  44.7 1.4 %fusion.22 = f32[8,128,256]{2,1,0:T(8,128)S(1)} fusion(bf16[8,128,128]{2,1,0:T(8,128)(2,1)S(1)} %fusion.4, bf16[8,128,256]{2,1,0:T(8,128)(2,1)} %copy-done.9, pred[8]{0:T(512)(128)(4,1)S(1)} %copy-done.20), kind=kOutput, calls=%fused_computation.54 | convolution fusion | flops 67371008 | bytes 1835016 | tf_op jit(solution)/shard_map/kab,kbr->kar/dot_general | solution.py:20
  46.1 1.4 %gather_fusion.7 = bf16[8,128,256]{2,1,0:T(8,128)(2,1)} fusion(bf16[2,128,256]{2,1,0:T(8,128)(2,1)S(1)} %bitcast.103, s32[1024]{0:T(1024)S(1)} %pad_clamp_fusion), kind=kCustom, calls=%fused_computation.7.clone | custom fusion | bytes 1048608 | tf_op jit(solution)/shard_map/jit(_take)/gather | solution.py:11
  47.5 0.6 copy-done.18
  48.1 0.1 copy-done.19
  48.2 1.5 %fusion.7 = bf16[8,128,128]{2,1,0:T(8,128)(2,1)S(1)} fusion(f32[8]{0:T(128)S(1)} %copy-done.30, bf16[1,4,1,8,128,128]{5,4,3,2,1,0:T(8,128)(2,1)} %param.12, bf16[8,128,256]{2,1,0:T(8,128)(2,1)S(1)} %gather_fusion.6, pred[8]{0:T(512)(128)(4,1)S(1)} %copy-done.19, bf16[8,128,256]{2,1,0:T(8,128)(2,1)} %gather_fusion.7, pred[8]{0:T(512)(128)(4,1)S(1)} %copy-done.18), kind=kOutput, calls=%fused_computation.22 | convolution fusion | flops 68157440 | bytes 1572912 | tf_op jit(solution)/shard_map/kar,kbr->kab/dot_general | solution.py:12
  49.7 1.4 %fusion.27 = f32[8,128,256]{2,1,0:T(8,128)} fusion(bf16[8,128,128]{2,1,0:T(8,128)(2,1)S(1)} %fusion.7, bf16[8,128,256]{2,1,0:T(8,128)(2,1)S(1)} %gather_fusion.6, pred[8]{0:T(512)(128)(4,1)S(1)} %copy-done.19), kind=kOutput, calls=%fused_computation.59 | convolution fusion | flops 67371008 | bytes 1835016 | tf_op jit(solution)/shard_map/kab,kar->kbr/dot_general | solution.py:23
  51.0 0.4 fusion.28
  51.4 0.6 copy-done.17
  52.0 1.2 fusion.12
  53.2 0.0 copy-done.5
  53.2 0.6 copy-done.29
  53.8 1.2 convolution_add_fusion.2
  55.0 0.6 copy-done.28
  55.6 1.2 convolution_add_fusion.1
  56.8 0.6 copy-done.27
  57.4 1.2 convolution_add_fusion
  58.6 1.3 copy.8
  59.9 0.2 reduce-scatter.2.cloned.1.call-start
  60.1 1.0 copy-done.2
  61.1 1.2 fusion.10
  62.3 0.7 copy-done.15
  63.0 1.2 fusion.9
  64.1 0.6 copy-done.14
  64.7 1.2 fusion.8
  66.0 1.1 copy-done.1
  67.1 1.2 fusion.11
  68.4 1.0 pad_maximum_fusion
  69.4 50.2 %all-reduce.2.cloned.1.call-done = f32[1024,256]{1,0:T(8,128)} async-done(((f32[1024,256]{1,0:T(8,128)}), f32[1024,256]{1,0:T(8,128)}) %all-reduce.2.cloned.1.call-update) | async-done | bytes 1048592 | tf_op jit(solution)/shard_map/psum | solution.py:88
  119.6 2.3 %copy.42 = f32[1024,256]{1,0:T(8,128)} copy(f32[1024,256]{1,0:T(8,128)} %all-reduce.2.cloned.1.call-done) | data formatting | bytes 2097152
  (71 shorter events, 0.4 us)
Async XLA Ops:
  8.0 13.1 %copy-start = (bf16[1024,256]{1,0:T(8,128)(2,1)S(1)}, bf16[1024,256]{1,0:T(8,128)(2,1)}, u32[]{:S(2)}) copy-start(bf16[1024,256]{1,0:T(8,128)(2,1)} %param.10) | copy-start | bytes 1572868
  8.0 111.6 %all-reduce.2.cloned.1.call-start = ((), (), s32[]{:S(2)}) async-start(), calls=%async_computation.1 | async-start | bytes 2097152 | tf_op jit(solution)/shard_map/psum | solution.py:88
  8.1 17.0 %collective-permute-start = (bf16[256,256]{1,0:T(8,128)(2,1)}, bf16[256,256]{1,0:T(8,128)(2,1)S(1)}, u32[]{:S(2)}, u32[]{:S(2)}) collective-permute-start(bf16[256,256]{1,0:T(8,128)(2,1)} %param.11), channel_id=1, source_target_pairs={{0,8},{8,16},{16,24},{24,0},{1,9},{9,17},{17,25},{25,1},{2,10},{10... | collective-permute-start | bytes 393224 | tf_op jit(solution)/shard_map/ppermute | solution.py:59
  11.0 15.0 %collective-permute-start.1 = (bf16[256,256]{1,0:T(8,128)(2,1)}, bf16[256,256]{1,0:T(8,128)(2,1)S(1)}, u32[]{:S(2)}, u32[]{:S(2)}) collective-permute-start(bf16[256,256]{1,0:T(8,128)(2,1)} %param.11), channel_id=1, source_target_pairs={{0,24},{8,0},{16,8},{24,16},{1,25},{9,1},{17,9},{25,17},{2,26},{10... | collective-permute-start | bytes 393224 | tf_op jit(solution)/shard_map/ppermute | solution.py:64
  12.1 1.3 %copy-start.12 = (s32[1,4,1,8]{3,2,1,0:T(1,128)S(1)}, s32[1,4,1,8]{3,2,1,0:T(1,128)}, u32[]{:S(2)}) copy-start(s32[1,4,1,8]{3,2,1,0:T(1,128)} %param.14) | copy-start | bytes 388
  12.1 1.3 %copy-start.13 = (s32[1,4,1,8]{3,2,1,0:T(1,128)S(1)}, s32[1,4,1,8]{3,2,1,0:T(1,128)}, u32[]{:S(2)}) copy-start(s32[1,4,1,8]{3,2,1,0:T(1,128)} %param.13) | copy-start | bytes 388
  14.0 17.6 %copy-start.24 = (pred[8]{0:T(512)(128)(4,1)}, pred[8]{0:T(512)(128)(4,1)S(1)}, u32[]{:S(2)}) copy-start(pred[8]{0:T(512)(128)(4,1)S(1)} %get-tuple-element.32) | copy-start | bytes 28
  14.0 17.6 %copy-start.26 = (pred[8]{0:T(512)(128)(4,1)}, pred[8]{0:T(512)(128)(4,1)S(1)}, u32[]{:S(2)}) copy-start(pred[8]{0:T(512)(128)(4,1)S(1)} %get-tuple-element.52) | copy-start | bytes 28
  14.6 0.7 copy-start.11
  17.8 0.9 copy-start.10
  25.0 5.9 %collective-permute-start.2 = (bf16[256,256]{1,0:T(8,128)(2,1)S(1)}, bf16[256,256]{1,0:T(8,128)(2,1)S(1)}, u32[]{:S(2)}, u32[]{:S(2)}) collective-permute-start(bf16[256,256]{1,0:T(8,128)(2,1)S(1)} %collective-permute-done), channel_id=1, source_target_pairs={{0,8},{8,16},{16,24},{24,0},{1,9},{9,17},{17,25},{25,1},{2,10},{10... | collective-permute-start | bytes 393224 | tf_op jit(solution)/shard_map/ppermute | solution.py:59
  32.9 1.0 copy-start.25
  35.3 1.0 copy-start.7
  35.9 0.7 copy-start.22
  35.9 0.7 copy-start.23
  35.9 0.7 copy-start.31
  40.6 1.0 copy-start.6
  41.2 2.1 %copy-start.9 = (bf16[8,128,256]{2,1,0:T(8,128)(2,1)}, bf16[8,128,256]{2,1,0:T(8,128)(2,1)S(1)}, u32[]{:S(2)}) copy-start(bf16[8,128,256]{2,1,0:T(8,128)(2,1)S(1)} %gather_fusion.1) | copy-start | bytes 1572868
  41.2 0.7 copy-start.20
  41.2 0.7 copy-start.21
  41.2 0.7 copy-start.32
  47.5 0.6 copy-start.18
  47.5 0.7 copy-start.19
  47.5 0.7 copy-start.30
  49.6 1.4 %copy-start.8 = (bf16[8,128,256]{2,1,0:T(8,128)(2,1)S(1)}, bf16[8,128,256]{2,1,0:T(8,128)(2,1)}, u32[]{:S(2)}) copy-start(bf16[8,128,256]{2,1,0:T(8,128)(2,1)} %gather_fusion.7) | copy-start | bytes 1572868
  51.4 0.6 copy-start.17
  52.0 1.2 copy-start.5
  53.2 0.6 copy-start.29
  53.8 1.2 copy-start.3
  55.0 0.6 copy-start.28
  56.8 0.6 copy-start.27
  59.9 1.2 copy-start.2
  59.9 1.2 copy-start.16
  59.9 59.7 %reduce-scatter.2.cloned.1.call-start = ((), (), s32[]{:S(2)}) async-start(), calls=%async_computation.2 | async-start | bytes 1310720 | tf_op jit(solution)/shard_map/reduce_scatter | solution.py:85
  61.1 3.0 %copy-start.4 = (f32[8,128,256]{2,1,0:T(8,128)S(1)}, f32[8,128,256]{2,1,0:T(8,128)}, u32[]{:S(2)}) copy-start(f32[8,128,256]{2,1,0:T(8,128)} %fusion.27) | copy-start | bytes 3145732
  62.3 0.7 copy-start.15
  64.1 0.6 copy-start.14
  65.9 1.2 copy-start.1
Sparse Core Ops, SparseCore 0:
  60.0 59.5 all-reduce.1
Sparse Core Ops, SparseCore 1:
  69.5 28.4 reduce-scatter.1
